TPU v7x, 32 devices: a whole 2x2x4 slice. The times are simulated.
32 devices in a mesh: row: 4 (over y, core), col: 8 (over z, x).
Axes of the slice: x: 2, y: 2, z: 4, core: 2. Of those that a mesh axis runs over, the one named last changes fastest.
Arguments:
- normal: float32 [16, 4, 256, 8, 8, 256], P(None, 'row', None, None, 'col'), may hold values from -1.5 to 1.5
- panel_inverse: float32 [256, 256], replicated, as said below
- rhs: float32 [16, 4, 256, 512], P(None, 'row', None, 'col'), may hold values from -0.009765625 to 0.009765625
- shifts: float32 [4], replicated, may hold values from 16 to 128
Outputs:
- schur: float32 [16, 4, 256, 8, 8, 256], P(None, 'row', None, None, 'col')
- eliminated: float32 [16, 4, 256, 512], P(None, 'row', None, 'col')
- applied: float32 [16, 4, 256, 512], P(None, 'row', None, 'col')
Inputs may be any that keep to these rules, and one draw needn't show every extreme that they name: `panel_inverse`: lower triangular with positive diagonal entries.
All inputs are finite; a program needn't handle non-finite values.
Results may differ from a plain program's by a relative error of at most 0.000076.
Values sent between devices are 32-bit elements; how exact they have to be, the bound alone decides.
A program may use at most 256 MiB of HBM per device.

v0:
```python
import jax
import jax.numpy as jnp
from jax import lax
from jax.sharding import PartitionSpec as P

R = 128


def spread_2(value, axis, source):
    kept = jnp.where(lax.axis_index(axis) == source, value, 0).astype(value.dtype)
    return lax.psum(kept, axis)


def pick_blocks(blocks, spacing, offset):
    grouped = blocks.reshape((blocks.shape[0] // spacing, spacing) + blocks.shape[1:])
    return lax.dynamic_index_in_dim(grouped, offset, 1, keepdims=False)


def shards(normal, panel_inverse, rhs, shifts):
    high = lax.Precision.HIGHEST
    row_index = lax.axis_index("row")
    col_index = lax.axis_index("col")
    nrow = lax.axis_size("row")
    ncol = lax.axis_size("col")
    spacing = ncol // nrow
    brows, nb, bcols = (normal.shape[0], normal.shape[2], normal.shape[3])
    narrow = rhs.shape[3]
    wide = narrow * ncol
    tile = normal.reshape(brows * nb, bcols * nb)
    owner = col_index % nrow
    offset = col_index // nrow
    local_panel = jnp.dot(
        tile[:, :nb], panel_inverse.T, precision=high, preferred_element_type=jnp.float32
    )
    panel = spread_2(local_panel, "col", 0)
    chosen = pick_blocks(panel.reshape(brows, nb, nb), spacing, offset)
    crossed = spread_2(chosen, "row", owner).reshape(bcols * nb, nb)
    updated = tile - jnp.dot(panel, crossed.T, precision=high, preferred_element_type=jnp.float32)
    leading = spread_2(rhs[0, 0], "row", 0)
    first = jnp.dot(panel_inverse, leading, precision=high, preferred_element_type=jnp.float32)
    reduced = rhs.reshape(brows * nb, narrow) - jnp.dot(
        panel, first, precision=high, preferred_element_type=jnp.float32
    )
    reduced = reduced.reshape(brows, nb, narrow)
    reduced = reduced.at[0].set(jnp.where(row_index == 0, first, reduced[0]))
    spread = lax.all_gather(reduced, "col", axis=2, tiled=True)
    scales = lax.dynamic_slice_in_dim(jnp.repeat(shifts, R), col_index * narrow, narrow)
    partial_value = lax.dot_general(
        updated,
        spread.reshape(brows * nb, wide),
        (((0,), (0,)), ((), ())),
        precision=high,
        preferred_element_type=jnp.float32,
    )
    totals = lax.psum(partial_value, "row")
    totals = totals.reshape(bcols, nb, ncol, narrow)
    arrived = lax.all_to_all(totals, "col", split_axis=2, concat_axis=2, tiled=True)
    arrived = arrived.reshape(bcols, nb, spacing, nrow, narrow)
    arrived = lax.dynamic_index_in_dim(arrived, row_index, 3, keepdims=False)
    product = jnp.transpose(arrived, (0, 2, 1, 3)).reshape(brows, nb, narrow)
    applied = product + reduced * scales[None, None, :]
    schur = updated.reshape(brows, 1, nb, bcols, 1, nb)
    return (schur, reduced.reshape(brows, 1, nb, narrow), applied.reshape(brows, 1, nb, narrow))


def solution(mesh):
    in_specs = (P(None, "row", None, None, "col", None), P(), P(None, "row", None, "col"), P())
    out_specs = (
        P(None, "row", None, None, "col", None),
        P(None, "row", None, "col"),
        P(None, "row", None, "col"),
    )
    return jax.shard_map(shards, mesh=mesh, in_specs=in_specs, out_specs=out_specs, check_vma=False)
```

profile of v0, /device:TPU:0, one launch (start us, length us, event | category | flops | bytes accessed | tf_op | source)
XLA Modules:
  0.0 758.9 jit_solution(6350466244515718778)
XLA Ops:
  7.2 0.0 copy-start
  7.2 0.0 all-reduce.5.cloned.1.call-start
  7.2 93.9 %reduce.2 = f32[16,256,8,256]{3,2,1,0:T(8,128)} reduce(f32[16,1,256,8,1,256]{5,4,3,2,1,0:T(1,128)} %param.6, f32[]{:T(128)} %constant.77), dimensions={1,4}, to_apply=%param.6.reduce_sub_computation | reduce | bytes 67108864 | tf_op args[0]
  101.1 29.9 %copy.37 = f32[512,8,8,256]{3,1,2,0:T(8,128)} copy(f32[512,8,8,256]{3,2,1,0:T(8,128)} %bitcast.49) | data formatting | bytes 67108864
  131.1 0.0 copy-done
  131.1 7.7 %convolution_select_fusion = f32[4096,256]{1,0:T(8,128)} fusion(f32[256,256]{1,0:T(8,128)S(1)} %copy-done, f32[4096,2048]{1,0:T(8,128)} %bitcast.47, pred[]{:T(512)S(6)} %eq.12), kind=kOutput, calls=%fused_computation.1 | convolution fusion | flops 3222274048 | bytes 8650753 | tf_op jit(solution)/shard_map/dot_general | solution.py:32
  138.7 0.0 copy-start.5
  138.7 0.0 all-reduce.5.cloned.1.call-update
  138.7 0.0 all-reduce.9.cloned.1.call-start
  138.8 1.1 copy-done.5
  139.9 0.6 select_bitcast_fusion
  140.6 157.4 %all-reduce.5.cloned.1.call-done = f32[4096,256]{1,0:T(8,128)} async-done(((f32[4096,256]{1,0:T(8,128)}), f32[4096,256]{1,0:T(8,128)}) %all-reduce.5.cloned.1.call-update) | async-done | bytes 4194320 | tf_op jit(solution)/shard_map/psum | solution.py:11
  298.0 3.1 dynamic-slice_select_fusion
  301.1 0.0 all-reduce.9.cloned.1.call-update
  301.1 0.5 all-gather.2.cloned.1.call-start
  301.6 0.1 copy.38
  301.7 51.0 %all-reduce.9.cloned.1.call-done = (f32[2048,256]{1,0:T(8,128)}, f32[256,64]{0,1:T(8,128)}) async-done(((f32[2048,256]{1,0:T(8,128)}, f32[256,64]{0,1:T(8,128)}), (f32[2048,256]{1,0:T(8,128)}, f32[256,64]{0,1:T(8,128)})) %all-reduce.9.cloned.1.call-update) | async-done | bytes 2162704 | tf_op jit(solution)/shard_map/psum | solution.py:11
  352.7 1.2 fusion.3
  354.0 6.5 convolution_subtract_fusion.1
  360.5 0.1 copy.27
  360.6 0.3 copy.39
  360.9 0.9 scatter.4
  361.8 0.0 copy-start.2
  361.8 1.0 copy-done.2
  362.8 0.0 all-gather.2.cloned.1.call-update
  362.8 0.0 all-reduce.7.cloned.1.call-start
  362.9 0.0 copy-done.4
  362.9 34.1 %convolution_subtract_fusion = f32[4096,2048]{1,0:T(8,128)} fusion(f32[4096,2048]{1,0:T(8,128)} %bitcast.48, f32[4096,256]{1,0:T(8,128)} %all-reduce.5.cloned.1.call-done, f32[2048,256]{1,0:T(8,128)S(1)} %copy-done.4), kind=kOutput, calls=%fused_computation | convolution fusion | flops 25778192384 | bytes 73400320 | tf_op jit(solution)/shard_map/dot_general | solution.py:38
  397.0 90.5 %all-gather.2.cloned.1.call-done = f32[16,256,512]{1,0,2:T(8,128)} async-done(((f32[16,256,64]{1,0,2:T(8,128)}), f32[16,256,512]{1,0,2:T(8,128)}) %all-gather.2.cloned.1.call-update) | async-done | bytes 8388624 | tf_op jit(solution)/shard_map/all_gather | solution.py:46
  487.5 9.9 %copy.28 = f32[16,256,512]{2,1,0:T(8,128)} copy(f32[16,256,512]{1,0,2:T(8,128)} %all-gather.2.cloned.1.call-done) | data formatting | bytes 16777216 | tf_op jit(solution)/shard_map/all_gather | solution.py:46
  497.4 64.5 %fusion.4 = f32[2048,512]{0,1:T(8,128)S(1)} fusion(f32[4096,2048]{1,0:T(8,128)} %convolution_subtract_fusion, f32[4096,512]{1,0:T(8,128)} %bitcast.55), kind=kOutput, calls=%fused_computation.13 | convolution fusion | flops 51539607552 | bytes 46137344 | tf_op jit(solution)/shard_map/dot_general | solution.py:48
  561.9 4.0 copy.40
  565.9 0.0 all-reduce.7.cloned.1.call-update
  565.9 0.0 copy-start.6
  565.9 83.8 %all-reduce.7.cloned.1.call-done = f32[8,256,8,64]{1,0,3,2:T(8,128)} async-done(((f32[8,256,8,64]{1,0,3,2:T(8,128)}), f32[8,256,8,64]{1,0,3,2:T(8,128)}) %all-reduce.7.cloned.1.call-update) | async-done | bytes 4194320 | tf_op jit(solution)/shard_map/psum | solution.py:55
  649.7 5.5 all-to-all-start
  655.2 0.0 copy-done.6
  655.2 0.1 broadcast_bitcast_fusion
  655.3 0.1 dynamic_slice.13
  655.4 48.4 %reshape.98 = f32[16,1,256,8,1,256]{5,4,3,2,1,0:T(1,128)} reshape(f32[4096,2048]{1,0:T(8,128)} %convolution_subtract_fusion) | data formatting | bytes 67108864 | tf_op jit(solution)/shard_map/reshape | solution.py:62
  703.8 0.0 copy-done.3
  703.8 1.6 copy.33
  705.4 42.8 %all-to-all-done = f32[8,256,8,64]{1,0,3,2:T(8,128)} async-done(((f32[8,256,8,64]{1,0,3,2:T(8,128)}), f32[8,256,8,64]{1,0,3,2:T(8,128)}, u32[]{:S(2)}, u32[]{:S(2)}) %all-to-all-start) | async-done | bytes 4194336 | tf_op jit(solution)/shard_map/all_to_all | solution.py:57
  748.2 1.3 constant_dynamic-slice_fusion
  749.6 0.3 copy.36
  749.9 0.7 fusion.1
  750.6 1.6 copy.34
  752.2 0.0 copy-done.1
  (4 shorter events, 0.0 us)
Async XLA Ops:
  7.2 123.9 %copy-start = (f32[256,256]{1,0:T(8,128)S(1)}, f32[256,256]{1,0:T(8,128)}, u32[]{:S(2)}) copy-start(f32[256,256]{1,0:T(8,128)} %param.7) | copy-start | bytes 786436
  7.2 290.8 %all-reduce.5.cloned.1.call-start = ((), (), s32[]{:S(2)}) async-start(), calls=%async_computation.1 | async-start | bytes 8388608 | tf_op jit(solution)/shard_map/psum | solution.py:11
  138.7 1.2 copy-start.5
  138.7 214.0 %all-reduce.9.cloned.1.call-start = ((), (), s32[]{:S(2)}) async-start(), calls=%async_computation.4 | async-start | bytes 4325376 | tf_op jit(solution)/shard_map/psum | solution.py:11
  301.1 186.4 %all-gather.2.cloned.1.call-start = ((), (), s32[]{:S(2)}) async-start(), calls=%async_computation.2 | async-start | bytes 9437184 | tf_op jit(solution)/shard_map/all_gather | solution.py:46
  354.0 8.9 %copy-start.4 = (f32[2048,256]{1,0:T(8,128)S(1)}, f32[2048,256]{1,0:T(8,128)}, u32[]{:S(2)}) copy-start(f32[2048,256]{1,0:T(8,128)} %get-tuple-element.27) | copy-start | bytes 6291460
  361.8 1.0 copy-start.2
  362.8 286.9 %all-reduce.7.cloned.1.call-start = ((), (), s32[]{:S(2)}) async-start(), calls=%async_computation.3 | async-start | bytes 8388608 | tf_op jit(solution)/shard_map/psum | solution.py:55
  565.9 89.3 %copy-start.6 = (f32[4]{0:T(128)S(1)}, f32[4]{0:T(128)}, u32[]{:S(2)}) copy-start(f32[4]{0:T(128)} %param.9) | copy-start | bytes 52
  649.7 98.5 %all-to-all-start = ((f32[8,256,8,64]{1,0,3,2:T(8,128)}), f32[8,256,8,64]{1,0,3,2:T(8,128)}, u32[]{:S(2)}, u32[]{:S(2)}) async-start(f32[8,256,8,64]{1,0,3,2:T(8,128)} %all-reduce.7.cloned.1.call-done), calls=%async_computation | async-start | bytes 8388608 | tf_op jit(solution)/shard_map/all_to_all | solution.py:57
  655.4 48.4 %copy-start.3 = (f32[16,256,64]{1,0,2:T(8,128)S(1)}, f32[16,256,64]{1,0,2:T(8,128)}, u32[]{:S(2)}) copy-start(f32[16,256,64]{1,0,2:T(8,128)} %copy-done.2) | copy-start | bytes 3145732
  748.2 3.9 copy-start.1
Sparse Core Ops, SparseCore 0:
  138.9 159.0 all-reduce.4
  301.2 51.4 all-reduce.8
  362.9 124.5 all-gather.1
  566.0 83.6 all-reduce.6
where the time goes:
time: 768 us; the launch traced here: 759 us
  waiting for transfers between devices  426 us (55%)
  matrix products  114 us (15%)
  local copies, waits for them, and re-layouts  101 us (13%)
  other arithmetic  98.3 us (13%)
  between operations  14.1 us (2%)
    psum x2, waiting for transfers between devices, spread_2(): return lax.psum(kept, axis)  208 us
    unnamed x1, other arithmetic  93.9 us
    all_gather x1, waiting for transfers between devices, shards(): spread = lax.all_gather(reduced, 'col', axis=2, tiled=True)  90.5 us
    psum x1, waiting for transfers between devices, shards(): totals = lax.psum(partial_value, 'row')  83.8 us
    dot_general x1, matrix products, shards(): lax.dot_general(updated, spread.reshape(brows * nb, wide), (((0,), (0,)),...  64.5 us
    reshape x1, local copies, waits for them, and re-layouts, shards(): schur = updated.reshape(brows, 1, nb, bcols, 1, nb)  48.4 us
    all_to_all x1, waiting for transfers between devices, shards(): lax.all_to_all(totals, 'col', split_axis=2, concat_axis=2, tiled=True)  42.8 us
    unnamed x21, local copies, waits for them, and re-layouts  39.9 us
  transfers between devices with their start and end apart: 5, of which 5 were waited for; matrix products, arithmetic and copies ran while one was open for 11% of the time, Pallas kernels for 0%

commit v1 on v0

--- a/solution.py
+++ b/solution.py
@@ -43,7 +43,16 @@
     )
     reduced = reduced.reshape(brows, nb, narrow)
     reduced = reduced.at[0].set(jnp.where(row_index == 0, first, reduced[0]))
-    spread = lax.all_gather(reduced, "col", axis=2, tiled=True)
+    world_n = jax.lax.axis_size("col")
+    k_now = reduced
+    chunks = [k_now]
+    later = sorted(((hop_no, (hop_no + 1) % world_n) for hop_no in range(world_n)))
+    for i in range(1, world_n):
+        k_now = jax.lax.ppermute(k_now, axis_name="col", perm=later)
+        chunks.insert(0, k_now)
+    earlier = jnp.concatenate(chunks, 2)
+    u_next = jax.lax.axis_index("col") + 1
+    spread = jnp.roll(earlier, u_next * reduced.shape[2], 2)
     scales = lax.dynamic_slice_in_dim(jnp.repeat(shifts, R), col_index * narrow, narrow)
     partial_value = lax.dot_general(
         updated,

time: 768 us -> 879 us (1.14)
  waiting for transfers between devices: 426 us -> 490 us
  local copies, waits for them, and re-layouts: 101 us -> 147 us
    ppermute x0 -> x7, waiting for transfers between devices: none -> 150 us  [shards(): k_now = jax.lax.ppermute(k_now, axis_name='col', perm=later)]
    all_gather x1 -> x0, waiting for transfers between devices: 90.5 us -> none  [shards(): spread = lax.all_gather(reduced, 'col', axis=2, tiled=True)]
    concatenate x0 -> x1, local copies, waits for them, and re-layouts: none -> 24.4 us  [shards(): spread = jnp.roll(earlier, u_next * reduced.shape[2], 2)]
    ppermute x0 -> x7, local copies, waits for them, and re-layouts: none -> 19.9 us  [shards(): k_now = jax.lax.ppermute(k_now, axis_name='col', perm=later)]
    all_gather x1 -> x0, local copies, waits for them, and re-layouts: 9.9 us -> none  [shards(): spread = lax.all_gather(reduced, 'col', axis=2, tiled=True)]
  transfers between devices with their start and end apart: 5 -> 11, of which waited for: 5 -> 10; matrix products, arithmetic and copies ran while one was open for 11% -> 12% of each run, Pallas kernels for 0% -> 0%
where the time goes in v1:
time: 879 us; the launch traced here: 869 us
  waiting for transfers between devices  490 us (56%)
  local copies, waits for them, and re-layouts  147 us (17%)
  matrix products  110 us (13%)
  other arithmetic  101 us (11%)
  between operations  14.1 us (2%)
    psum x2, waiting for transfers between devices, spread_2(): return lax.psum(kept, axis)  209 us
    ppermute x7, waiting for transfers between devices, shards(): k_now = jax.lax.ppermute(k_now, axis_name='col', perm=later)  150 us
    unnamed x1, other arithmetic  93.9 us
    psum x1, waiting for transfers between devices, shards(): totals = lax.psum(partial_value, 'row')  87.5 us
    dot_general x1, matrix products, shards(): lax.dot_general(updated, spread.reshape(brows * nb, wide), (((0,), (0,)),...  59.9 us
    reshape x1, local copies, waits for them, and re-layouts, shards(): schur = updated.reshape(brows, 1, nb, bcols, 1, nb)  48.3 us
    all_to_all x1, waiting for transfers between devices, shards(): lax.all_to_all(totals, 'col', split_axis=2, concat_axis=2, tiled=True)  42.9 us
    unnamed x21, local copies, waits for them, and re-layouts  42.8 us
  transfers between devices with their start and end apart: 11, of which 10 were waited for; matrix products, arithmetic and copies ran while one was open for 12% of the time, Pallas kernels for 0%

profile of v1, /device:TPU:0, one launch (start us, length us, event | category | flops | bytes accessed | tf_op | source)
XLA Modules:
  0.0 868.8 jit_solution(846632964294410241)
XLA Ops:
  7.2 93.9 %reduce.2 = f32[16,256,8,256]{3,2,1,0:T(8,128)} reduce(f32[16,1,256,8,1,256]{5,4,3,2,1,0:T(1,128)} %param.6, f32[]{:T(128)} %constant.98), dimensions={1,4}, to_apply=%param.6.reduce_sub_computation | reduce | bytes 67108864 | tf_op args[0]
  101.1 30.0 %copy.44 = f32[512,8,8,256]{3,1,2,0:T(8,128)} copy(f32[512,8,8,256]{3,2,1,0:T(8,128)} %bitcast.46) | data formatting | bytes 67108864
  131.1 7.7 convolution_select_fusion
  138.9 1.1 copy-done.2
  140.0 0.6 select_bitcast_fusion
  140.6 157.4 %all-reduce.5.cloned.1.call-done = f32[4096,256]{1,0:T(8,128)} async-done(((f32[4096,256]{1,0:T(8,128)}), f32[4096,256]{1,0:T(8,128)}) %all-reduce.5.cloned.1.call-update) | async-done | bytes 4194320 | tf_op jit(solution)/shard_map/psum | solution.py:11
  298.1 3.1 dynamic-slice_select_fusion
  301.2 0.2 all-reduce.7.cloned.1.call-start
  301.4 0.1 copy.45
  301.5 51.3 %all-reduce.9.cloned.1.call-done = (f32[2048,256]{1,0:T(8,128)}, f32[256,64]{0,1:T(8,128)}) async-done(((f32[2048,256]{1,0:T(8,128)}, f32[256,64]{0,1:T(8,128)}), (f32[2048,256]{1,0:T(8,128)}, f32[256,64]{0,1:T(8,128)})) %all-reduce.9.cloned.1.call-update) | async-done | bytes 2162704 | tf_op jit(solution)/shard_map/psum | solution.py:11
  352.8 1.2 fusion.2
  354.0 6.3 convolution_subtract_fusion.1
  360.4 0.6 copy.43
  361.0 0.1 copy.21
  361.1 1.6 copy.22
  362.7 1.5 collective-permute-start
  364.1 26.1 %collective-permute-done = f32[16,256,64]{1,2,0:T(8,128)S(1)} collective-permute-done((f32[16,256,64]{1,2,0:T(8,128)}, f32[16,256,64]{1,2,0:T(8,128)S(1)}, u32[]{:S(2)}, u32[]{:S(2)}) %collective-permute-start) | collective-permute-done | bytes 1048608 | tf_op jit(solution)/shard_map/ppermute | solution.py:51
  390.2 26.5 %collective-permute-done.1 = f32[16,256,64]{1,2,0:T(8,128)S(1)} collective-permute-done((f32[16,256,64]{1,2,0:T(8,128)S(1)}, f32[16,256,64]{1,2,0:T(8,128)S(1)}, u32[]{:S(2)}, u32[]{:S(2)}) %collective-permute-start.1) | collective-permute-done | bytes 1048608 | tf_op jit(solution)/shard_map/ppermute | solution.py:51
  416.7 1.0 copy-done.3
  417.7 25.6 %collective-permute-done.2 = f32[16,256,64]{1,2,0:T(8,128)S(1)} collective-permute-done((f32[16,256,64]{1,2,0:T(8,128)S(1)}, f32[16,256,64]{1,2,0:T(8,128)S(1)}, u32[]{:S(2)}, u32[]{:S(2)}) %collective-permute-start.2) | collective-permute-done | bytes 1048608 | tf_op jit(solution)/shard_map/ppermute | solution.py:51
  443.3 1.0 copy-done.4
  444.3 24.8 %collective-permute-done.3 = f32[16,256,64]{1,2,0:T(8,128)S(1)} collective-permute-done((f32[16,256,64]{1,2,0:T(8,128)S(1)}, f32[16,256,64]{1,2,0:T(8,128)S(1)}, u32[]{:S(2)}, u32[]{:S(2)}) %collective-permute-start.3) | collective-permute-done | bytes 1048608 | tf_op jit(solution)/shard_map/ppermute | solution.py:51
  469.1 1.0 copy-done.5
  470.1 24.0 %collective-permute-done.4 = f32[16,256,64]{1,2,0:T(8,128)} collective-permute-done((f32[16,256,64]{1,2,0:T(8,128)S(1)}, f32[16,256,64]{1,2,0:T(8,128)}, u32[]{:S(2)}, u32[]{:S(2)}) %collective-permute-start.4) | collective-permute-done | bytes 1048608 | tf_op jit(solution)/shard_map/ppermute | solution.py:51
  494.1 23.4 %collective-permute-done.5 = f32[16,256,64]{1,2,0:T(8,128)} collective-permute-done((f32[16,256,64]{1,2,0:T(8,128)}, f32[16,256,64]{1,2,0:T(8,128)}, u32[]{:S(2)}, u32[]{:S(2)}) %collective-permute-start.5) | collective-permute-done | bytes 1048608 | tf_op jit(solution)/shard_map/ppermute | solution.py:51
  517.5 34.7 %convolution_subtract_fusion = f32[4096,2048]{1,0:T(8,128)} fusion(f32[4096,2048]{1,0:T(8,128)} %bitcast.45, f32[4096,256]{1,0:T(8,128)} %all-reduce.5.cloned.1.call-done, f32[2048,256]{1,0:T(8,128)} %get-tuple-element.24), kind=kOutput, calls=%fused_computation | convolution fusion | flops 25778192384 | bytes 73400320 | tf_op jit(solution)/shard_map/dot_general | solution.py:38
  552.2 2.0 copy.29
  554.2 3.3 copy.28
  557.4 3.1 copy.27
  560.6 2.0 copy.26
  562.6 3.1 copy.25
  565.7 3.2 copy.24
  568.9 3.2 copy.23
  572.1 24.4 %concatenate.8 = f32[16,256,1024]{2,1,0:T(8,128)} concatenate(f32[16,256,64]{2,1,0:T(8,128)} %copy.23, f32[16,256,64]{2,1,0:T(8,128)} %copy.24, f32[16,256,64]{2,1,0:T(8,128)} %copy.25, f32[16,256,64]{2,1,0:T(8,128)} %copy.26, f32[16,256,64]{2,1,0:T(8,128)} %copy.27, f32[16,256,64]{2,1,0:T(8,128)} %copy.28, f32[16,256,64]{2,1,0:T(8,128)} %copy.29, ...), dimensions={2} | concatenate | bytes 33554432 | tf_op jit(solution)/shard_map/jit(_roll_dynamic)/concatenate | solution.py:55
  596.5 6.2 constant_dynamic-slice_fusion.1
  602.7 59.9 %fusion.3 = f32[2048,512]{0,1:T(8,128)S(1)} fusion(f32[4096,2048]{1,0:T(8,128)} %convolution_subtract_fusion, f32[4096,512]{1,0:T(8,128)S(1)} %bitcast.51), kind=kOutput, calls=%fused_computation.14 | convolution fusion | flops 51539607552 | bytes 46137344 | tf_op jit(solution)/shard_map/dot_general | solution.py:57
  662.6 4.0 copy.46
  666.6 87.5 %all-reduce.7.cloned.1.call-done = f32[8,256,8,64]{1,0,3,2:T(8,128)} async-done(((f32[8,256,8,64]{1,0,3,2:T(8,128)}), f32[8,256,8,64]{1,0,3,2:T(8,128)}) %all-reduce.7.cloned.1.call-update) | async-done | bytes 4194320 | tf_op jit(solution)/shard_map/psum | solution.py:64
  754.0 5.5 all-to-all-start
  759.5 0.1 broadcast_bitcast_fusion
  759.6 0.1 dynamic_slice.18
  759.7 48.3 %reshape.98 = f32[16,1,256,8,1,256]{5,4,3,2,1,0:T(1,128)} reshape(f32[4096,2048]{1,0:T(8,128)} %convolution_subtract_fusion) | data formatting | bytes 67108864 | tf_op jit(solution)/shard_map/reshape | solution.py:71
  808.0 1.6 copy.40
  809.6 42.9 %all-to-all-done = f32[8,256,8,64]{1,0,3,2:T(8,128)} async-done(((f32[8,256,8,64]{1,0,3,2:T(8,128)}), f32[8,256,8,64]{1,0,3,2:T(8,128)}, u32[]{:S(2)}, u32[]{:S(2)}) %all-to-all-start) | async-done | bytes 4194336 | tf_op jit(solution)/shard_map/all_to_all | solution.py:66
  852.5 1.3 constant_dynamic-slice_fusion
  853.8 2.0 copy.38
  855.8 3.1 bitcast_add_fusion
  859.0 3.1 copy.41
  (26 shorter events, 0.2 us)
Async XLA Ops:
  7.2 123.9 %copy-start = (f32[256,256]{1,0:T(8,128)S(1)}, f32[256,256]{1,0:T(8,128)}, u32[]{:S(2)}) copy-start(f32[256,256]{1,0:T(8,128)} %param.7) | copy-start | bytes 786436
  7.2 290.9 %all-reduce.5.cloned.1.call-start = ((), (), s32[]{:S(2)}) async-start(), calls=%async_computation.1 | async-start | bytes 8388608 | tf_op jit(solution)/shard_map/psum | solution.py:11
  138.8 1.2 copy-start.2
  138.8 214.0 %all-reduce.9.cloned.1.call-start = ((), (), s32[]{:S(2)}) async-start(), calls=%async_computation.3 | async-start | bytes 4325376 | tf_op jit(solution)/shard_map/psum | solution.py:11
  301.2 452.8 %all-reduce.7.cloned.1.call-start = ((), (), s32[]{:S(2)}) async-start(), calls=%async_computation.2 | async-start | bytes 8388608 | tf_op jit(solution)/shard_map/psum | solution.py:64
  362.7 27.6 %collective-permute-start = (f32[16,256,64]{1,2,0:T(8,128)}, f32[16,256,64]{1,2,0:T(8,128)S(1)}, u32[]{:S(2)}, u32[]{:S(2)}) collective-permute-start(f32[16,256,64]{1,2,0:T(8,128)} %copy.22), channel_id=1, source_target_pairs={{0,1},{1,2},{2,3},{3,4},{4,5},{5,6},{6,7},{7,0},{8,9},{9,10},{10,1... | collective-permute-start | bytes 3145736 | tf_op jit(solution)/shard_map/ppermute | solution.py:51
  390.2 26.5 %collective-permute-start.1 = (f32[16,256,64]{1,2,0:T(8,128)S(1)}, f32[16,256,64]{1,2,0:T(8,128)S(1)}, u32[]{:S(2)}, u32[]{:S(2)}) collective-permute-start(f32[16,256,64]{1,2,0:T(8,128)S(1)} %collective-permute-done), channel_id=1, source_target_pairs={{0,1},{1,2},{2,3},{3,4},{4,5},{5,6},{6,7},{7,0},{8,9},{9,10},{10,1... | collective-permute-start | bytes 3145736 | tf_op jit(solution)/shard_map/ppermute | solution.py:51
  416.7 1.0 copy-start.3
  417.7 25.6 %collective-permute-start.2 = (f32[16,256,64]{1,2,0:T(8,128)S(1)}, f32[16,256,64]{1,2,0:T(8,128)S(1)}, u32[]{:S(2)}, u32[]{:S(2)}) collective-permute-start(f32[16,256,64]{1,2,0:T(8,128)S(1)} %collective-permute-done.1), channel_id=1, source_target_pairs={{0,1},{1,2},{2,3},{3,4},{4,5},{5,6},{6,7},{7,0},{8,9},{9,10},{10,1... | collective-permute-start | bytes 3145736 | tf_op jit(solution)/shard_map/ppermute | solution.py:51
  443.3 1.0 copy-start.4
  444.3 24.8 %collective-permute-start.3 = (f32[16,256,64]{1,2,0:T(8,128)S(1)}, f32[16,256,64]{1,2,0:T(8,128)S(1)}, u32[]{:S(2)}, u32[]{:S(2)}) collective-permute-start(f32[16,256,64]{1,2,0:T(8,128)S(1)} %collective-permute-done.2), channel_id=1, source_target_pairs={{0,1},{1,2},{2,3},{3,4},{4,5},{5,6},{6,7},{7,0},{8,9},{9,10},{10,1... | collective-permute-start | bytes 3145736 | tf_op jit(solution)/shard_map/ppermute | solution.py:51
  469.1 1.0 copy-start.5
  470.1 24.0 %collective-permute-start.4 = (f32[16,256,64]{1,2,0:T(8,128)S(1)}, f32[16,256,64]{1,2,0:T(8,128)}, u32[]{:S(2)}, u32[]{:S(2)}) collective-permute-start(f32[16,256,64]{1,2,0:T(8,128)S(1)} %collective-permute-done.3), channel_id=1, source_target_pairs={{0,1},{1,2},{2,3},{3,4},{4,5},{5,6},{6,7},{7,0},{8,9},{9,10},{10,1... | collective-permute-start | bytes 3145736 | tf_op jit(solution)/shard_map/ppermute | solution.py:51
  494.1 23.4 %collective-permute-start.5 = (f32[16,256,64]{1,2,0:T(8,128)}, f32[16,256,64]{1,2,0:T(8,128)}, u32[]{:S(2)}, u32[]{:S(2)}) collective-permute-start(f32[16,256,64]{1,2,0:T(8,128)} %collective-permute-done.4), channel_id=1, source_target_pairs={{0,1},{1,2},{2,3},{3,4},{4,5},{5,6},{6,7},{7,0},{8,9},{9,10},{10,1... | collective-permute-start | bytes 3145736 | tf_op jit(solution)/shard_map/ppermute | solution.py:51
  517.5 51.4 %collective-permute-start.6 = (f32[16,256,64]{1,2,0:T(8,128)}, f32[16,256,64]{1,2,0:T(8,128)}, u32[]{:S(2)}, u32[]{:S(2)}) collective-permute-start(f32[16,256,64]{1,2,0:T(8,128)} %collective-permute-done.5), channel_id=1, source_target_pairs={{0,1},{1,2},{2,3},{3,4},{4,5},{5,6},{6,7},{7,0},{8,9},{9,10},{10,1... | collective-permute-start | bytes 3145736 | tf_op jit(solution)/shard_map/ppermute | solution.py:51
  554.1 6.4 copy-start.6
  666.5 93.0 %copy-start.7 = (f32[4]{0:T(128)S(1)}, f32[4]{0:T(128)}, u32[]{:S(2)}) copy-start(f32[4]{0:T(128)} %param.9) | copy-start | bytes 52
  754.0 98.5 %all-to-all-start = ((f32[8,256,8,64]{1,0,3,2:T(8,128)}), f32[8,256,8,64]{1,0,3,2:T(8,128)}, u32[]{:S(2)}, u32[]{:S(2)}) async-start(f32[8,256,8,64]{1,0,3,2:T(8,128)} %all-reduce.7.cloned.1.call-done), calls=%async_computation | async-start | bytes 8388608 | tf_op jit(solution)/shard_map/all_to_all | solution.py:66
  853.8 8.3 copy-start.1
Sparse Core Ops, SparseCore 0:
  138.9 159.1 all-reduce.4
  301.3 51.4 all-reduce.8
  666.7 87.3 all-reduce.6
